TPU v7x, 512 devices: a whole 4x8x8 slice. The times are simulated.
512 devices in a mesh: utt: 8 (over x, core), tm: 64 (over y, z).
Axes of the slice: x: 4, y: 8, z: 8, core: 2. Of those that a mesh axis runs over, the one named last changes fastest.
Arguments:
- phone_ids: int32 [8, 4096], P('utt', 'tm'), may hold values from 0 to 255
- durations: int32 [8, 4096], P('utt'), may hold values from 1 to 16, 16384 in all within a row
- utt_lengths: int32 [8, 64], P('utt'), may hold values from 1 to 256, 4096 in all within a row
- utt_order: int32 [8, 64], P('utt'), may hold values from 0 to 63, each once within a row
- buckets: int32 [8, 64, 8], P('utt', 'tm'), may hold values from 0 to 7, each once within a row
- embed_table: bfloat16 [256, 384], replicated, may hold values from -6 to 6
- conv1_weight: bfloat16 [3456, 768], P(None, 'tm'), may hold values from -0.109375 to 0.109375
- conv2_weight: bfloat16 [384, 768], P(None, 'tm'), may hold values from -0.21875 to 0.21875
- norm_gain: float32 [384], replicated, may hold values from 0.1 to 1.9
- mel_weight: bfloat16 [384, 80], replicated, may hold values from -0.3125 to 0.3125
- pre_weight: bfloat16 [7, 80, 512], replicated, may hold values from -0.25 to 0.25
- up_weight: bfloat16 [512, 16, 256], P('tm'), may hold values from -0.1875 to 0.1875
Outputs:
- bucketed: bfloat16 [8, 64, 8, 256, 256], P('utt', 'tm')
All inputs are finite; a program needn't handle non-finite values.
Results may differ from a plain program's by a relative error of at most 0.0067.
Values may be sent and summed in bfloat16 or wider, within the bound.
A program may use at most 64 MiB of HBM per device.

v0:
```python
import jax
import jax.numpy as jnp
from jax import lax
from jax.sharding import PartitionSpec as P

F_DEV = 256
EPS = 1e-05


def padded(cells, sides, width):
    for axis, dim in sides:
        count = lax.axis_size(axis)
        ends = count - 1
        head = lax.slice_in_dim(cells, 0, width, axis=dim)
        tail = lax.slice_in_dim(cells, cells.shape[dim] - width, cells.shape[dim], axis=dim)
        cells = jnp.concatenate(
            [
                lax.ppermute(tail, axis, [(i, (i + 1) % count) for i in range(ends)]),
                cells,
                lax.ppermute(head, axis, [((i + 1) % count, i) for i in range(ends)]),
            ],
            axis=dim,
        )
    return cells


def utterance_of(indices, bounds):
    return jnp.sum((bounds[None, :] <= indices[:, None]).astype(jnp.int32), axis=1)


def frame_layout(lasting, lengths, ordering):
    phone_total = lasting.shape[0]
    utt_count = lengths.shape[0]
    phone_index = jnp.arange(phone_total, dtype=jnp.int32)
    bounds = jnp.cumsum(lengths)
    utt_first = bounds - lengths
    owners = utterance_of(phone_index, bounds)
    inclusive = jnp.cumsum(lasting)
    exclusive = inclusive - lasting
    first_frame = jnp.take(exclusive, utt_first)
    utt_frames = jnp.take(inclusive, bounds - 1) - first_frame
    slots = jnp.arange(utt_count, dtype=jnp.int32)
    places = jnp.sum(jnp.where(ordering[None, :] == slots[:, None], slots[None, :], 0), axis=1)
    offsets = jnp.sum(jnp.where(places[None, :] < places[:, None], utt_frames[None, :], 0), axis=1)
    starting = jnp.take(offsets, owners) + exclusive - jnp.take(first_frame, owners)
    return (starting, owners, bounds)


def masked_unfold(row_block, labels, offset, amount, width_taps, reach):
    center = labels[offset : offset + amount]
    columns = []
    for tap in range(width_taps):
        anchor = offset - reach + tap
        keep = (labels[anchor : anchor + amount] == center)[:, None]
        columns.append(
            jnp.where(keep, row_block[anchor : anchor + amount], jnp.zeros((), row_block.dtype))
        )
    return jnp.concatenate(columns, axis=1)


def shards(
    phone_ids,
    durations,
    utt_lengths,
    utt_order,
    buckets,
    embed_table,
    conv1_weight,
    conv2_weight,
    norm_gain,
    mel_weight,
    pre_weight,
    up_weight,
):
    phone_count = phone_ids.shape[1]
    device = lax.axis_index("tm")
    lasting = durations[0]
    starting, owners, bounds = frame_layout(lasting, utt_lengths[0], utt_order[0])
    ending = starting + lasting
    nearby = device * phone_count + jnp.arange(-4, phone_count + 4, dtype=jnp.int32)
    phone_labels = jnp.where(nearby < 0, -1, utterance_of(nearby, bounds))
    symbols = embed_table.shape[0]
    choose = (phone_ids[0][:, None] == jnp.arange(symbols, dtype=jnp.int32)[None, :]).astype(
        jnp.bfloat16
    )
    embedded = jnp.dot(choose, embed_table, preferred_element_type=jnp.float32).astype(jnp.bfloat16)
    widened = padded(embedded, (("tm", 0),), 4)
    unfolded = masked_unfold(widened, phone_labels, 4, phone_count, 9, 4)
    inward = lax.all_gather(conv1_weight, "tm", axis=1, tiled=True)
    outward = lax.all_gather(conv2_weight, "tm", axis=1, tiled=True)
    filters = jnp.maximum(
        jnp.dot(unfolded, inward, preferred_element_type=jnp.float32), 0.0
    ).astype(jnp.bfloat16)
    conv_out = lax.dot_general(
        filters, outward, (((1,), (1,)), ((), ())), preferred_element_type=jnp.float32
    )
    resid = embedded.astype(jnp.float32) + conv_out
    center = jnp.mean(resid, axis=1, keepdims=True)
    spread = jnp.mean((resid - center) ** 2, axis=1, keepdims=True)
    decoded = ((resid - center) * lax.rsqrt(spread + EPS) * norm_gain[None, :]).astype(jnp.bfloat16)
    span = F_DEV + 8
    frames = device * F_DEV - 4 + jnp.arange(span, dtype=jnp.int32)
    mel_width = mel_weight.shape[1]
    portion = lax.all_gather(decoded, "tm", axis=0, tiled=True)
    hit = (frames[:, None] >= starting[None, :]) & (frames[:, None] < ending[None, :])
    sums = jnp.dot(hit.astype(jnp.bfloat16), portion, preferred_element_type=jnp.float32)
    marks = jnp.sum(jnp.where(hit, owners[None, :] + 1, 0), axis=1)
    sums, marks = (sums, marks)
    mel_frames = jnp.dot(
        sums.astype(jnp.bfloat16), mel_weight, preferred_element_type=jnp.float32
    ).astype(jnp.bfloat16)
    frame_labels = marks - 1
    channels = pre_weight.shape[2]
    pre_flat = pre_weight.reshape(7 * mel_width, channels)
    columns = masked_unfold(mel_frames, frame_labels, 4, F_DEV, 7, 3)
    summed = jnp.dot(columns, pre_flat, preferred_element_type=jnp.float32)
    act_wide = padded(
        jnp.where(summed >= 0, summed, 0.1 * summed).astype(jnp.bfloat16), (("tm", 0),), 1
    )
    center_labels = frame_labels[4 : 4 + F_DEV]
    same_prev = (frame_labels[3 : 3 + F_DEV] == center_labels)[:, None]
    same_next = (frame_labels[5 : 5 + F_DEV] == center_labels)[:, None]
    act_mid = act_wide[1 : F_DEV + 1]
    act_prev = jnp.where(same_prev, act_wide[0:F_DEV], jnp.zeros((), jnp.bfloat16))
    act_next = jnp.where(same_next, act_wide[2 : F_DEV + 2], jnp.zeros((), jnp.bfloat16))
    out_width = up_weight.shape[2]
    groups = lax.axis_size("utt")
    placing = buckets[0, 0]
    selector = (placing[None, :] == jnp.arange(groups, dtype=jnp.int32)[:, None]).astype(
        jnp.bfloat16
    )
    portion = lax.all_gather(up_weight, "tm", axis=0, tiled=True)
    amount = portion.shape[0]
    weights = portion.reshape(amount, 16 * out_width)
    middle = jnp.dot(
        act_mid, weights[:, 4 * out_width : 12 * out_width], preferred_element_type=jnp.float32
    )
    before = jnp.dot(act_prev, weights[:, 12 * out_width :], preferred_element_type=jnp.float32)
    after = jnp.dot(act_next, weights[:, : 4 * out_width], preferred_element_type=jnp.float32)
    upsampled = middle + jnp.concatenate([before, after], axis=1)
    segments = upsampled.astype(jnp.bfloat16).reshape(groups, -1, out_width)
    outgoing = jnp.einsum(
        "bj,jsc->bsc", selector, segments, preferred_element_type=jnp.float32
    ).astype(jnp.bfloat16)
    arrived = lax.all_to_all(outgoing, "utt", split_axis=0, concat_axis=0, tiled=True)
    return arrived.reshape(1, 1, groups, -1, out_width)


def solution(mesh):
    placed = (
        P("utt", "tm"),
        P("utt", None),
        P("utt", None),
        P("utt", None),
        P("utt", "tm", None),
        P(),
        P(None, "tm"),
        P(None, "tm"),
        P(),
        P(),
        P(),
        P("tm", None, None),
    )
    return jax.shard_map(
        shards,
        mesh=mesh,
        in_specs=placed,
        out_specs=P("utt", "tm", None, None, None),
        check_vma=False,
    )
```

profile of v0, /device:TPU:1, one launch (start us, length us, event | category | flops | bytes accessed | tf_op | source)
XLA Modules:
  0.0 333.1 jit_solution(16332967862284316481)
XLA Ops:
  6.5 0.7 all-gather.10.cloned.1.call-update
  7.3 1.1 convolution_convert_fusion.1
  8.5 4.8 %collective-permute-start = (bf16[4,384]{1,0:T(4,128)(2,1)S(1)}, bf16[4,384]{1,0:T(4,128)(2,1)S(1)}, u32[]{:S(2)}, u32[]{:S(2)}) collective-permute-start(bf16[4,384]{1,0:T(4,128)(2,1)S(1)} %get-tuple-element.16), channel_id=1, source_target_pairs={{0,1},{1,2},{2,3},{3,4},{4,5},{5,6},{6,7},{7,8},{8,9},{9,10},{10,1... | collective-permute-start | bytes 9224 | tf_op jit(solution)/shard_map/ppermute | solution.py:18
  13.3 1.3 collective-permute-start.1
  14.6 0.7 copy.22
  15.7 48.4 %all-gather.1 = bf16[64,12,384]{2,1,0:T(8,128)(2,1)S(1)} all-gather(bf16[1,12,384]{2,1,0:T(8,128)(2,1)} %bitcast.173), channel_id=1, replica_groups=mesh['utt'=8,'tm'=64] {'tm'}, dimensions={0}, use_global_device_ids=true | all-gather | bytes 599040 | tf_op jit(solution)/shard_map/all_gather | solution.py:90
  65.0 44.1 %all-gather.10.cloned.1.call-done = bf16[64,12,3456]{2,1,0:T(8,128)(2,1)} async-done(((bf16[1,12,3456]{2,1,0:T(8,128)(2,1)}), bf16[64,12,3456]{2,1,0:T(8,128)(2,1)}) %all-gather.10.cloned.1.call-update) | async-done | bytes 5308432 | tf_op jit(solution)/shard_map/all_gather | solution.py:89
  109.1 9.2 %reshape.279 = bf16[768,3456]{1,0:T(8,128)(2,1)} reshape(bf16[64,12,3456]{2,1,0:T(8,128)(2,1)} %all-gather.10.cloned.1.call-done) | data formatting | bytes 10616832
  118.4 4.6 %fusion.79 = (f32[64]{0:T(128)S(1)}, f32[64,384]{1,0:T(8,128)S(1)}) fusion(bf16[768,384]{1,0:T(8,128)(2,1)S(1)} %reshape.281, bf16[64,3456]{1,0:T(8,128)(2,1)S(1)} %fusion.48, bf16[768,3456]{1,0:T(8,128)(2,1)} %reshape.279, bf16[64,384]{1,0:T(8,128)(2,1)S(1)} %convolution_convert_fusion.1), kind=kOutput, calls=%fused_computation.146 | convolution fusion | flops 377659328 | bytes 6488320 | tf_op jit(solution)/shard_map/dot_general | solution.py:94
  123.1 0.7 multiply_convert_fusion
  123.9 0.7 all-gather.8.cloned.1.call-update
  125.3 0.8 gather_fusion.1
  126.0 0.8 gather_fusion
  127.1 0.7 fusion.74
  128.5 0.7 fusion.73
  129.2 0.7 fusion.72
  129.9 0.7 fusion.71
  130.6 0.7 fusion.76
  131.4 0.7 fusion.75
  132.1 0.7 fusion.77
  133.0 80.0 %fusion.67 = (s32[4096]{0:T(1024)S(1)}, s32[4096]{0:T(1024)S(1)}) fusion(s32[4096]{0:T(1024)S(1)} %bitcast.171, s32[]{:T(128)} %bitcast.135, s32[]{:T(128)} %bitcast.134, s32[]{:T(128)} %bitcast.133, s32[]{:T(128)} %bitcast.132, s32[]{:T(128)} %bitcast.131, s32[]{:T(128)} %bitcast.130, s32[]{:T(128)} %bitcast.129, s32[]{:T(128)} %bitcast.128, s32[]{:T(128)} %bitcast.127, ...), kind=kLoop, calls=%fused_computation.134 | loop fusion | flops 819200 | bytes 82432 | tf_op jit(solution)/shard_map/add | solution.py:79
  213.1 0.9 select_reduce_fusion
  214.1 3.4 %fusion.11 = bf16[264,80]{0,1:T(8,128)(2,1)S(1)} fusion(bf16[384,80]{0,1:T(8,128)(2,1)S(1)} %copy-done.5, bf16[4096,384]{1,0:T(8,128)(2,1)} %all-gather.6.cloned.1.call-done, s32[4096]{0:T(1024)S(1)} %get-tuple-element.6, s32[4096]{0:T(1024)S(1)} %get-tuple-element.8, s32[264]{0:T(512)S(1)} %iota_add_fusion), kind=kOutput, calls=%fused_computation.19 | convolution fusion | flops 850058880 | bytes 3283232 | tf_op jit(solution)/shard_map/dot_general | solution.py:109
  218.6 1.3 collective-permute-start.2
  219.8 69.4 %all-gather.8.cloned.1.call-done = bf16[512,16,256]{2,1,0:T(8,128)(2,1)} async-done(((bf16[8,16,256]{2,1,0:T(8,128)(2,1)}), bf16[512,16,256]{2,1,0:T(8,128)(2,1)}) %all-gather.8.cloned.1.call-update) | async-done | bytes 4194320 | tf_op jit(solution)/shard_map/all_gather | solution.py:132
  289.2 4.4 %copy.25 = bf16[64,8,16,256]{3,1,2,0:T(8,128)(2,1)S(1)} copy(bf16[64,8,16,256]{3,2,1,0:T(8,128)(2,1)} %bitcast.164) | data formatting | bytes 8388608
  293.6 1.5 collective-permute-start.3
  295.6 2.4 collective-permute-done.3
  298.5 0.7 fusion.1
  299.7 0.7 convolution_convert_fusion
  300.7 25.0 %all_to_all.5 = bf16[8,256,256]{2,1,0:T(8,128)(2,1)S(1)} all-to-all(bf16[8,256,256]{2,1,0:T(8,128)(2,1)S(1)} %copy.24), channel_id=1, replica_groups=mesh['utt'=8,'tm'=64] {'utt'}, dimensions={0} | all-to-all | bytes 2097152 | tf_op jit(solution)/shard_map/all_to_all | solution.py:145
  325.6 1.0 copy.43
  (71 shorter events, 6.1 us)
Async XLA Ops:
  6.5 211.6 %copy-start = (bf16[7,80,512]{2,1,0:T(8,128)(2,1)S(1)}, bf16[7,80,512]{2,1,0:T(8,128)(2,1)}, u32[]{:S(2)}) copy-start(bf16[7,80,512]{2,1,0:T(8,128)(2,1)} %param.26) | copy-start | bytes 1720324
  6.5 102.6 %all-gather.10.cloned.1.call-start = ((), (), s32[]{:S(2)}) async-start(), calls=%async_computation.3 | async-start | bytes 7188480 | tf_op jit(solution)/shard_map/all_gather | solution.py:89
  7.3 206.8 %all-gather.6.cloned.1.call-start = ((), (), s32[]{:S(2)}) async-start(), calls=%async_computation.1 | async-start | bytes 3194880 | tf_op jit(solution)/shard_map/all_gather | solution.py:104
  8.5 55.8 %collective-permute-start = (bf16[4,384]{1,0:T(4,128)(2,1)S(1)}, bf16[4,384]{1,0:T(4,128)(2,1)S(1)}, u32[]{:S(2)}, u32[]{:S(2)}) collective-permute-start(bf16[4,384]{1,0:T(4,128)(2,1)S(1)} %get-tuple-element.16), channel_id=1, source_target_pairs={{0,1},{1,2},{2,3},{3,4},{4,5},{5,6},{6,7},{7,8},{8,9},{9,10},{10,1... | collective-permute-start | bytes 9224 | tf_op jit(solution)/shard_map/ppermute | solution.py:18
  13.3 51.3 %collective-permute-start.1 = (bf16[4,384]{1,0:T(4,128)(2,1)S(1)}, bf16[4,384]{1,0:T(4,128)(2,1)S(1)}, u32[]{:S(2)}, u32[]{:S(2)}) collective-permute-start(bf16[4,384]{1,0:T(4,128)(2,1)S(1)} %get-tuple-element.15), channel_id=1, source_target_pairs={{1,0},{2,1},{3,2},{4,3},{5,4},{6,5},{7,6},{8,7},{9,8},{10,9},{11,1... | collective-permute-start | bytes 9224 | tf_op jit(solution)/shard_map/ppermute | solution.py:20
  118.3 4.8 %copy-start.2 = (f32[384]{0:T(512)S(1)}, f32[384]{0:T(512)}, u32[]{:S(2)}) copy-start(f32[384]{0:T(512)} %param.24) | copy-start | bytes 4612
  118.3 6.3 %copy-start.1 = (s32[1,4096]{1,0:T(1,128)S(1)}, s32[1,4096]{1,0:T(1,128)}, u32[]{:S(2)}) copy-start(s32[1,4096]{1,0:T(1,128)} %param.17) | copy-start | bytes 49156
  118.3 6.7 %copy-start.3 = (s32[1,64]{1,0:T(1,128)S(1)}, s32[1,64]{1,0:T(1,128)}, u32[]{:S(2)}) copy-start(s32[1,64]{1,0:T(1,128)} %param.18) | copy-start | bytes 772
  118.3 8.5 %copy-start.6 = (s32[1,64]{1,0:T(1,128)S(1)}, s32[1,64]{1,0:T(1,128)}, u32[]{:S(2)}) copy-start(s32[1,64]{1,0:T(1,128)} %param.19) | copy-start | bytes 772
  118.3 95.8 %copy-start.5 = (bf16[384,80]{0,1:T(8,128)(2,1)S(1)}, bf16[384,80]{0,1:T(8,128)(2,1)}, u32[]{:S(2)}) copy-start(bf16[384,80]{0,1:T(8,128)(2,1)} %param.25) | copy-start | bytes 184324
  123.9 165.4 %all-gather.8.cloned.1.call-start = ((), (), s32[]{:S(2)}) async-start(), calls=%async_computation.2 | async-start | bytes 4259840 | tf_op jit(solution)/shard_map/all_gather | solution.py:132
  218.6 76.6 %collective-permute-start.2 = (bf16[1,512]{1,0:T(2,128)(2,1)S(1)}, bf16[1,512]{1,0:T(2,128)(2,1)S(1)}, u32[]{:S(2)}, u32[]{:S(2)}) collective-permute-start(bf16[1,512]{1,0:T(2,128)(2,1)S(1)} %get-tuple-element.13), channel_id=1, source_target_pairs={{0,1},{1,2},{2,3},{3,4},{4,5},{5,6},{6,7},{7,8},{8,9},{9,10},{10,1... | collective-permute-start | bytes 3080 | tf_op jit(solution)/shard_map/ppermute | solution.py:18
  293.6 4.3 %collective-permute-start.3 = (bf16[1,512]{1,0:T(2,128)(2,1)S(1)}, bf16[1,512]{1,0:T(2,128)(2,1)S(1)}, u32[]{:S(2)}, u32[]{:S(2)}) collective-permute-start(bf16[1,512]{1,0:T(2,128)(2,1)S(1)} %get-tuple-element.14), channel_id=1, source_target_pairs={{1,0},{2,1},{3,2},{4,3},{5,4},{6,5},{7,6},{8,7},{9,8},{10,9},{11,1... | collective-permute-start | bytes 3080 | tf_op jit(solution)/shard_map/ppermute | solution.py:20
  298.5 1.3 copy-start.4
Sparse Core Ops, SparseCore 0:
  10.4 98.6 all-gather.9
  124.0 79.0 all-gather.5
  206.1 83.0 all-gather.7
where the time goes:
time: 335 us; the launch traced here: 333 us
  waiting for transfers between devices  117 us (35%)
  other arithmetic  84.5 us (25%)
  blocking collectives  73.4 us (22%)
  local copies, waits for them, and re-layouts  23.8 us (7%)
  between operations  13.5 us (4%)
  matrix products  11.9 us (4%)
  starting transfers between devices  8.95 us (3%)
    add x1, other arithmetic, shards(): ending = starting + lasting  80 us
    all_gather x1, waiting for transfers between devices, shards(): portion = lax.all_gather(up_weight, 'tm', axis=0, tiled=True)  69.4 us
    all_gather x1, blocking collectives, shards(): outward = lax.all_gather(conv2_weight, 'tm', axis=1, tiled=True)  48.4 us
    all_gather x1, waiting for transfers between devices, shards(): inward = lax.all_gather(conv1_weight, 'tm', axis=1, tiled=True)  44.1 us
    all_to_all x1, blocking collectives, shards(): lax.all_to_all(outgoing, 'utt', split_axis=0, concat_axis=0, tiled=True)  25 us
    unnamed x20, local copies, waits for them, and re-layouts  14.8 us
  transfers between devices with their start and end apart: 7, of which 3 were waited for; matrix products, arithmetic and copies ran while one was open for 31% of the time, Pallas kernels for 0%

commit v1 on v0

--- a/solution.py
+++ b/solution.py
@@ -87,7 +87,9 @@
     widened = padded(embedded, (("tm", 0),), 4)
     unfolded = masked_unfold(widened, phone_labels, 4, phone_count, 9, 4)
     inward = lax.all_gather(conv1_weight, "tm", axis=1, tiled=True)
-    outward = lax.all_gather(conv2_weight, "tm", axis=1, tiled=True)
+    outward = jnp.concatenate(
+        lax.all_to_all(jnp.stack([conv2_weight] * lax.axis_size("tm")), "tm", 0, 0), axis=1
+    )
     filters = jnp.maximum(
         jnp.dot(unfolded, inward, preferred_element_type=jnp.float32), 0.0
     ).astype(jnp.bfloat16)

time: 335 us -> 347 us (1.036)
  blocking collectives: 73.4 us -> 25 us
  waiting for transfers between devices: 117 us -> 159 us
  starting transfers between devices: 8.95 us -> 26.4 us
    all_gather x1 -> x0, blocking collectives: 48.4 us -> none  [shards(): outward = lax.all_gather(conv2_weight, 'tm', axis=1, tiled=True)]
    all_to_all x0 -> x1, waiting for transfers between devices: none -> 21 us  [shards(): lax.all_to_all(jnp.stack([conv2_weight] * lax.axis_size('tm')), 'tm', 0, 0)]
    all_gather x1, waiting for transfers between devices: 44.1 us -> 64.5 us  [shards(): inward = lax.all_gather(conv1_weight, 'tm', axis=1, tiled=True)]
    all_to_all x0 -> x1, starting transfers between devices: none -> 17.5 us  [shards(): lax.all_to_all(jnp.stack([conv2_weight] * lax.axis_size('tm')), 'tm', 0, 0)]
    unnamed x20 -> x19, local copies, waits for them, and re-layouts: 14.8 us -> 14.7 us
  transfers between devices with their start and end apart: 7 -> 8, of which waited for: 3 -> 4; matrix products, arithmetic and copies ran while one was open for 31% -> 30% of each run, Pallas kernels for 0% -> 0%
where the time goes in v1:
time: 347 us; the launch traced here: 345 us
  waiting for transfers between devices  159 us (46%)
  other arithmetic  84.5 us (24%)
  starting transfers between devices  26.4 us (8%)
  local copies, waits for them, and re-layouts  25.4 us (7%)
  blocking collectives  25 us (7%)
  between operations  13.5 us (4%)
  matrix products  11.9 us (3%)
    add x1, other arithmetic, shards(): ending = starting + lasting  80 us
    all_gather x1, waiting for transfers between devices, shards(): portion = lax.all_gather(up_weight, 'tm', axis=0, tiled=True)  69.4 us
    all_gather x1, waiting for transfers between devices, shards(): inward = lax.all_gather(conv1_weight, 'tm', axis=1, tiled=True)  64.5 us
    all_to_all x1, blocking collectives, shards(): lax.all_to_all(outgoing, 'utt', split_axis=0, concat_axis=0, tiled=True)  25 us
    all_to_all x1, waiting for transfers between devices, shards(): lax.all_to_all(jnp.stack([conv2_weight] * lax.axis_size('tm')), 'tm', 0, 0)  21 us
    all_to_all x1, starting transfers between devices, shards(): lax.all_to_all(jnp.stack([conv2_weight] * lax.axis_size('tm')), 'tm', 0, 0)  17.5 us
    unnamed x19, local copies, waits for them, and re-layouts  14.7 us
  transfers between devices with their start and end apart: 8, of which 4 were waited for; matrix products, arithmetic and copies ran while one was open for 30% of the time, Pallas kernels for 0%

profile of v1, /device:TPU:1, one launch (start us, length us, event | category | flops | bytes accessed | tf_op | source)
XLA Modules:
  0.0 345.4 jit_solution(12016876565271888409)
XLA Ops:
  6.5 0.7 all-gather.9.cloned.1.call-update
  7.3 1.1 convolution_convert_fusion.1
  8.4 4.8 %collective-permute-start = (bf16[4,384]{1,0:T(4,128)(2,1)S(1)}, bf16[4,384]{1,0:T(4,128)(2,1)S(1)}, u32[]{:S(2)}, u32[]{:S(2)}) collective-permute-start(bf16[4,384]{1,0:T(4,128)(2,1)S(1)} %get-tuple-element.16), channel_id=1, source_target_pairs={{0,1},{1,2},{2,3},{3,4},{4,5},{5,6},{6,7},{7,8},{8,9},{9,10},{10,1... | collective-permute-start | bytes 9224 | tf_op jit(solution)/shard_map/ppermute | solution.py:18
  13.2 1.3 collective-permute-start.1
  14.5 1.7 stack.2
  16.2 17.5 %all-to-all-start = ((bf16[64,384,12]{1,2,0:T(8,128)(2,1)}), bf16[64,384,12]{1,2,0:T(8,128)(2,1)S(1)}, u32[]{:S(2)}, u32[]{:S(2)}) async-start(bf16[64,384,12]{1,2,0:T(8,128)(2,1)} %stack.2), calls=%async_computation | async-start | bytes 1572864 | tf_op jit(solution)/shard_map/all_to_all | solution.py:91
  33.7 0.7 copy.23
  35.7 21.0 %all-to-all-done = bf16[64,384,12]{1,2,0:T(8,128)(2,1)S(1)} async-done(((bf16[64,384,12]{1,2,0:T(8,128)(2,1)}), bf16[64,384,12]{1,2,0:T(8,128)(2,1)S(1)}, u32[]{:S(2)}, u32[]{:S(2)}) %all-to-all-start) | async-done | bytes 589856 | tf_op jit(solution)/shard_map/all_to_all | solution.py:91
  56.8 64.5 %all-gather.9.cloned.1.call-done = bf16[64,12,3456]{2,1,0:T(8,128)(2,1)} async-done(((bf16[1,12,3456]{2,1,0:T(8,128)(2,1)}), bf16[64,12,3456]{2,1,0:T(8,128)(2,1)}) %all-gather.9.cloned.1.call-update) | async-done | bytes 5308432 | tf_op jit(solution)/shard_map/all_gather | solution.py:89
  121.3 9.2 %reshape.289 = bf16[768,3456]{1,0:T(8,128)(2,1)} reshape(bf16[64,12,3456]{2,1,0:T(8,128)(2,1)} %all-gather.9.cloned.1.call-done) | data formatting | bytes 10616832
  130.5 4.6 %fusion.79 = (f32[64]{0:T(128)S(1)}, f32[64,384]{1,0:T(8,128)S(1)}) fusion(bf16[384,768]{0,1:T(8,128)(2,1)S(1)} %reshape.121, bf16[64,3456]{1,0:T(8,128)(2,1)S(1)} %fusion.48, bf16[768,3456]{1,0:T(8,128)(2,1)} %reshape.289, bf16[64,384]{1,0:T(8,128)(2,1)S(1)} %convolution_convert_fusion.1), kind=kOutput, calls=%fused_computation.146 | convolution fusion | flops 377659328 | bytes 6488320 | tf_op jit(solution)/shard_map/dot_general | solution.py:96
  135.3 0.7 multiply_convert_fusion
  137.5 0.8 gather_fusion.1
  138.2 0.8 gather_fusion
  140.7 0.7 fusion.73
  141.4 0.7 fusion.72
  142.1 0.7 fusion.71
  142.8 0.7 fusion.76
  143.6 0.7 fusion.75
  144.3 0.7 fusion.77
  145.2 80.0 %fusion.67 = (s32[4096]{0:T(1024)S(1)}, s32[4096]{0:T(1024)S(1)}) fusion(s32[4096]{0:T(1024)S(1)} %bitcast.172, s32[]{:T(128)} %bitcast.135, s32[]{:T(128)} %bitcast.134, s32[]{:T(128)} %bitcast.133, s32[]{:T(128)} %bitcast.132, s32[]{:T(128)} %bitcast.131, s32[]{:T(128)} %bitcast.130, s32[]{:T(128)} %bitcast.129, s32[]{:T(128)} %bitcast.128, s32[]{:T(128)} %bitcast.127, ...), kind=kLoop, calls=%fused_computation.134 | loop fusion | flops 819200 | bytes 82432 | tf_op jit(solution)/shard_map/add | solution.py:79
  225.3 0.9 select_reduce_fusion
  226.3 3.4 fusion.11
  230.7 1.3 collective-permute-start.2
  232.0 69.4 %all-gather.7.cloned.1.call-done = bf16[512,16,256]{2,1,0:T(8,128)(2,1)} async-done(((bf16[8,16,256]{2,1,0:T(8,128)(2,1)}), bf16[512,16,256]{2,1,0:T(8,128)(2,1)}) %all-gather.7.cloned.1.call-update) | async-done | bytes 4194320 | tf_op jit(solution)/shard_map/all_gather | solution.py:134
  301.4 4.4 %copy.26 = bf16[64,8,16,256]{3,1,2,0:T(8,128)(2,1)S(1)} copy(bf16[64,8,16,256]{3,2,1,0:T(8,128)(2,1)} %bitcast.164) | data formatting | bytes 8388608
  305.8 1.5 collective-permute-start.3
  307.8 2.4 collective-permute-done.3
  310.7 0.7 fusion.1
  311.9 0.7 convolution_convert_fusion
  312.9 25.0 %all_to_all.10 = bf16[8,256,256]{2,1,0:T(8,128)(2,1)S(1)} all-to-all(bf16[8,256,256]{2,1,0:T(8,128)(2,1)S(1)} %copy.25), channel_id=1, replica_groups=mesh['utt'=8,'tm'=64] {'utt'}, dimensions={0} | all-to-all | bytes 2097152 | tf_op jit(solution)/shard_map/all_to_all | solution.py:147
  337.9 1.0 copy.44
  (73 shorter events, 7.5 us)
Async XLA Ops:
  6.5 223.8 %copy-start = (bf16[7,80,512]{2,1,0:T(8,128)(2,1)S(1)}, bf16[7,80,512]{2,1,0:T(8,128)(2,1)}, u32[]{:S(2)}) copy-start(bf16[7,80,512]{2,1,0:T(8,128)(2,1)} %param.26) | copy-start | bytes 1720324
  6.5 114.7 %all-gather.9.cloned.1.call-start = ((), (), s32[]{:S(2)}) async-start(), calls=%async_computation.4 | async-start | bytes 7188480 | tf_op jit(solution)/shard_map/all_gather | solution.py:89
  8.4 26.5 %collective-permute-start = (bf16[4,384]{1,0:T(4,128)(2,1)S(1)}, bf16[4,384]{1,0:T(4,128)(2,1)S(1)}, u32[]{:S(2)}, u32[]{:S(2)}) collective-permute-start(bf16[4,384]{1,0:T(4,128)(2,1)S(1)} %get-tuple-element.16), channel_id=1, source_target_pairs={{0,1},{1,2},{2,3},{3,4},{4,5},{5,6},{6,7},{7,8},{8,9},{9,10},{10,1... | collective-permute-start | bytes 9224 | tf_op jit(solution)/shard_map/ppermute | solution.py:18
  13.2 22.0 %collective-permute-start.1 = (bf16[4,384]{1,0:T(4,128)(2,1)S(1)}, bf16[4,384]{1,0:T(4,128)(2,1)S(1)}, u32[]{:S(2)}, u32[]{:S(2)}) collective-permute-start(bf16[4,384]{1,0:T(4,128)(2,1)S(1)} %get-tuple-element.15), channel_id=1, source_target_pairs={{1,0},{2,1},{3,2},{4,3},{5,4},{6,5},{7,6},{8,7},{9,8},{10,9},{11,1... | collective-permute-start | bytes 9224 | tf_op jit(solution)/shard_map/ppermute | solution.py:20
  16.2 40.5 %all-to-all-start = ((bf16[64,384,12]{1,2,0:T(8,128)(2,1)}), bf16[64,384,12]{1,2,0:T(8,128)(2,1)S(1)}, u32[]{:S(2)}, u32[]{:S(2)}) async-start(bf16[64,384,12]{1,2,0:T(8,128)(2,1)} %stack.2), calls=%async_computation | async-start | bytes 1572864 | tf_op jit(solution)/shard_map/all_to_all | solution.py:91
  33.7 192.6 %all-gather.5.cloned.1.call-start = ((), (), s32[]{:S(2)}) async-start(), calls=%async_computation.2 | async-start | bytes 3194880 | tf_op jit(solution)/shard_map/all_gather | solution.py:106
  130.5 4.8 %copy-start.2 = (f32[384]{0:T(512)S(1)}, f32[384]{0:T(512)}, u32[]{:S(2)}) copy-start(f32[384]{0:T(512)} %param.24) | copy-start | bytes 4612
  130.5 6.3 %copy-start.1 = (s32[1,4096]{1,0:T(1,128)S(1)}, s32[1,4096]{1,0:T(1,128)}, u32[]{:S(2)}) copy-start(s32[1,4096]{1,0:T(1,128)} %param.17) | copy-start | bytes 49156
  130.5 6.7 %copy-start.3 = (s32[1,64]{1,0:T(1,128)S(1)}, s32[1,64]{1,0:T(1,128)}, u32[]{:S(2)}) copy-start(s32[1,64]{1,0:T(1,128)} %param.18) | copy-start | bytes 772
  130.5 8.5 %copy-start.6 = (s32[1,64]{1,0:T(1,128)S(1)}, s32[1,64]{1,0:T(1,128)}, u32[]{:S(2)}) copy-start(s32[1,64]{1,0:T(1,128)} %param.19) | copy-start | bytes 772
  130.5 95.8 %copy-start.5 = (bf16[384,80]{0,1:T(8,128)(2,1)S(1)}, bf16[384,80]{0,1:T(8,128)(2,1)}, u32[]{:S(2)}) copy-start(bf16[384,80]{0,1:T(8,128)(2,1)} %param.25) | copy-start | bytes 184324
  136.1 165.4 %all-gather.7.cloned.1.call-start = ((), (), s32[]{:S(2)}) async-start(), calls=%async_computation.3 | async-start | bytes 4259840 | tf_op jit(solution)/shard_map/all_gather | solution.py:134
  230.7 76.6 %collective-permute-start.2 = (bf16[1,512]{1,0:T(2,128)(2,1)S(1)}, bf16[1,512]{1,0:T(2,128)(2,1)S(1)}, u32[]{:S(2)}, u32[]{:S(2)}) collective-permute-start(bf16[1,512]{1,0:T(2,128)(2,1)S(1)} %get-tuple-element.13), channel_id=1, source_target_pairs={{0,1},{1,2},{2,3},{3,4},{4,5},{5,6},{6,7},{7,8},{8,9},{9,10},{10,1... | collective-permute-start | bytes 3080 | tf_op jit(solution)/shard_map/ppermute | solution.py:18
  305.8 4.3 %collective-permute-start.3 = (bf16[1,512]{1,0:T(2,128)(2,1)S(1)}, bf16[1,512]{1,0:T(2,128)(2,1)S(1)}, u32[]{:S(2)}, u32[]{:S(2)}) collective-permute-start(bf16[1,512]{1,0:T(2,128)(2,1)S(1)} %get-tuple-element.14), channel_id=1, source_target_pairs={{1,0},{2,1},{3,2},{4,3},{5,4},{6,5},{7,6},{8,7},{9,8},{10,9},{11,1... | collective-permute-start | bytes 3080 | tf_op jit(solution)/shard_map/ppermute | solution.py:20
  310.7 1.3 copy-start.4
Sparse Core Ops, SparseCore 0:
  10.4 110.8 all-gather.8
  136.2 79.0 all-gather.4
  218.3 83.0 all-gather.6
